TPU v7x, 32 devices: a whole 2x2x4 slice. The times are simulated.
32 devices in a mesh: scene: 2 (over y), seq: 4 (over z), head: 2 (over x), band: 2 (over core).
Axes of the slice: x: 2, y: 2, z: 4, core: 2. Of those that a mesh axis runs over, the one named last changes fastest.
Arguments:
- tokens: bfloat16 [8, 12, 37, 1024], P(('scene', 'seq'), ('head', 'band')), parts along dimension 0, may hold values from -6 to 6
- frame_gain: float32 [1024], replicated, may hold values from 0.5 to 1.5
- frame_qkv: bfloat16 [3, 1024, 1024], P(None, None, 'head'), may hold values from -6 to 6
- frame_out: bfloat16 [1024, 1024], P('head'), may hold values from -0.1875 to 0.1875
- global_gain: float32 [1024], replicated, may hold values from 0.5 to 1.5
- global_qkv: bfloat16 [3, 1024, 1024], P(None, None, 'head'), may hold values from -6 to 6
- global_out: bfloat16 [1024, 1024], P('head'), may hold values from -0.1875 to 0.1875
- head_gain: float32 [2048], replicated, may hold values from 0.5 to 1.5
- head_proj: bfloat16 [2048, 256], replicated, may hold values from -0.125 to 0.125
- head_bias: float32 [256], replicated, may hold values from -3 to 3
- head_conv: bfloat16 [3, 3, 256, 256], replicated, may hold values from -0.125 to 0.125
Outputs:
- blocks: bfloat16 [8, 12, 37, 1024], P(('scene', 'seq'), ('head', 'band')), parts along dimension 0
- features: bfloat16 [8, 12, 37, 256], P(('scene', 'seq'), ('head', 'band')), parts along dimension 0
There are 2 independent parts, one for each index of `scene`. A program takes and returns all parts, laid end to end along the dimension named above; an argument that names none is the same for every part. Nothing has to cross between parts.
All inputs are finite; a program needn't handle non-finite values.
Results may differ from a plain program's by a relative error of at most 0.017.
Values may be sent and summed in bfloat16 or wider, within the bound.
A program may use at most 256 MiB of HBM per device.

v0:
```python
import jax
import jax.numpy as jnp
from jax import lax
from jax.sharding import PartitionSpec as P

HD = 64
norm_eps = 1e-06
head_eps = 1e-05


def padded_2(block, sides, width):
    for axis, dim in sides:
        count = lax.axis_size(axis)
        forward = [(i, i + 1) for i in range(count - 1)]
        backward = [(target, source) for source, target in forward]
        low = lax.ppermute(
            lax.slice_in_dim(block, block.shape[dim] - width, None, axis=dim), axis, forward
        )
        high = lax.ppermute(lax.slice_in_dim(block, 0, width, axis=dim), axis, backward)
        block = jnp.concatenate([low, block, high], axis=dim)
    return block


def layer_norm(values, gain, epsilon):
    centre = values - jnp.mean(values, axis=-1, keepdims=True)
    spread = jnp.mean(centre * centre, axis=-1, keepdims=True)
    return centre * lax.rsqrt(spread + epsilon) * gain


def by_heads(matrix):
    return matrix.reshape(matrix.shape[0], matrix.shape[1] // HD, HD)


def attend_local(queries, keys_all, values_all):
    scores = jnp.einsum(
        "qhd,khd->qhk", by_heads(queries), by_heads(keys_all), preferred_element_type=jnp.float32
    ) * HD ** (-0.5)
    probs = jnp.exp(scores - jnp.max(scores, axis=-1, keepdims=True))
    mixed = jnp.einsum(
        "qhk,khd->qhd",
        probs.astype(jnp.bfloat16),
        by_heads(values_all),
        preferred_element_type=jnp.float32,
    )
    mixed = mixed / jnp.sum(probs, axis=-1)[..., None]
    return mixed.reshape(queries.shape).astype(jnp.bfloat16)


def key_step(local_rows, portion_rows):
    amount = portion_rows // local_rows
    best = 1
    for factor in range(1, amount + 1):
        if amount % factor == 0 and local_rows * factor <= max(local_rows, 1024):
            best = factor
    return local_rows * best


def fresh_carry(queries):
    heads_q = by_heads(queries)
    return (
        jnp.full(heads_q.shape[:2], -jnp.inf, jnp.float32),
        jnp.zeros(heads_q.shape[:2], jnp.float32),
        jnp.zeros(heads_q.shape, jnp.float32),
    )


def finish(carry, queries):
    return (carry[2] / carry[1][..., None]).reshape(queries.shape).astype(jnp.bfloat16)


def fold_keys(queries, carry, portions, local_rows):
    keys_in, values_in = portions
    step_rows = key_step(local_rows, keys_in.shape[0])
    heads_q = by_heads(queries)
    key_blocks = keys_in.reshape(-1, step_rows, keys_in.shape[1])
    value_blocks = values_in.reshape(-1, step_rows, values_in.shape[1])

    def absorb(states, blocks_pair):
        running_max, running_sum, weighted = states
        scores = jnp.einsum(
            "qhd,khd->qhk", heads_q, by_heads(blocks_pair[0]), preferred_element_type=jnp.float32
        ) * HD ** (-0.5)
        new_max = jnp.maximum(running_max, jnp.max(scores, axis=-1))
        decay = jnp.exp(running_max - new_max)
        probs = jnp.exp(scores - new_max[..., None])
        running_sum = running_sum * decay + jnp.sum(probs, axis=-1)
        weighted = weighted * decay[..., None] + jnp.einsum(
            "qhk,khd->qhd",
            probs.astype(jnp.bfloat16),
            by_heads(blocks_pair[1]),
            preferred_element_type=jnp.float32,
        )
        return ((new_max, running_sum, weighted), None)

    carry, ignored = lax.scan(absorb, carry, (key_blocks, value_blocks))
    return carry


def attention_block(inputs, gain, qkv_weight, out_weight, wide):
    normed = layer_norm(inputs.astype(jnp.float32), gain, norm_eps).astype(jnp.bfloat16)
    gathered = lax.all_gather(normed, "head", axis=1, tiled=True)
    flattened = gathered.reshape(-1, gathered.shape[-1])
    query_rows = jnp.dot(flattened, qkv_weight[0], preferred_element_type=jnp.float32).astype(
        jnp.bfloat16
    )
    key_rows = jnp.dot(flattened, qkv_weight[1], preferred_element_type=jnp.float32).astype(
        jnp.bfloat16
    )
    value_rows = jnp.dot(flattened, qkv_weight[2], preferred_element_type=jnp.float32).astype(
        jnp.bfloat16
    )
    if wide:
        carry = fold_keys(
            query_rows,
            fresh_carry(query_rows),
            (
                lax.all_gather(key_rows, ("seq", "band"), axis=0, tiled=True),
                lax.all_gather(value_rows, ("seq", "band"), axis=0, tiled=True),
            ),
            key_rows.shape[0],
        )
        attended = finish(carry, query_rows)
    else:
        keys_all, values_all = (
            lax.all_gather(key_rows, "band", axis=0, tiled=True),
            lax.all_gather(value_rows, "band", axis=0, tiled=True),
        )
        attended = attend_local(query_rows, keys_all, values_all)
    band_rows = inputs.shape[1] * inputs.shape[2]
    own_rows = lax.all_to_all(attended, "head", split_axis=0, concat_axis=1, tiled=True)
    branch = jnp.dot(
        own_rows,
        lax.all_gather(out_weight, "head", axis=0, tiled=True),
        preferred_element_type=jnp.float32,
    )
    merged = inputs.astype(jnp.float32).reshape(band_rows, -1) + branch
    return merged.astype(jnp.bfloat16).reshape(inputs.shape)


def on_device(
    tokens,
    frame_gain,
    frame_qkv,
    frame_out,
    global_gain,
    global_qkv,
    global_out,
    head_gain,
    head_proj,
    head_bias,
    head_conv,
):
    first = attention_block(tokens, frame_gain, frame_qkv, frame_out, False)
    second = attention_block(first, global_gain, global_qkv, global_out, True)
    band_height = tokens.shape[1]
    grid_width = tokens.shape[2]
    stacked = jnp.concatenate([first.astype(jnp.float32), second.astype(jnp.float32)], axis=-1)
    normed = layer_norm(stacked, head_gain, head_eps).astype(jnp.bfloat16)
    projected = (
        jnp.dot(
            normed.reshape(-1, stacked.shape[-1]), head_proj, preferred_element_type=jnp.float32
        )
        + head_bias
    )
    projected = projected.astype(jnp.bfloat16).reshape(
        tokens.shape[0], band_height, grid_width, head_proj.shape[1]
    )
    padded = padded_2(projected, ((("head", "band"), 1),), 1)
    padded = jnp.pad(padded, ((0, 0), (0, 0), (1, 1), (0, 0)))
    totals = jnp.zeros(projected.shape, jnp.float32)
    for offset_row in range(3):
        for offset_col in range(3):
            window = padded[
                :, offset_row : offset_row + band_height, offset_col : offset_col + grid_width
            ]
            totals = totals + jnp.einsum(
                "frcx,xy->frcy",
                window,
                head_conv[offset_row, offset_col],
                preferred_element_type=jnp.float32,
            )
    return (second, totals.astype(jnp.bfloat16))


def solution(mesh):
    return jax.shard_map(
        on_device,
        mesh=mesh,
        in_specs=(
            P(("scene", "seq"), ("head", "band"), None, None),
            P(),
            P(None, None, "head"),
            P("head", None),
            P(),
            P(None, None, "head"),
            P("head", None),
            P(),
            P(),
            P(),
            P(),
        ),
        out_specs=(
            P(("scene", "seq"), ("head", "band"), None, None),
            P(("scene", "seq"), ("head", "band"), None, None),
        ),
        check_vma=False,
    )
```

profile of v0, /device:TPU:1, one launch (start us, length us, event | category | flops | bytes accessed | tf_op | source)
XLA Modules:
  0.0 186.9 jit_solution(2766687566238518207)
XLA Ops:
  11.3 8.4 %all_gather.24 = bf16[1,6,37,1024]{3,2,0,1:T(8,128)(2,1)S(1)} all-gather(bf16[1,3,37,1024]{3,2,0,1:T(8,128)(2,1)S(1)} %multiply_convert_fusion.1), channel_id=1, replica_groups=mesh['scene'=2,'seq'=4,'head'=2,'band'=2] {'head'}, dimensions={1}, use_global_device_ids=true | all-gather | bytes 681984 | tf_op jit(solution)/shard_map/all_gather | solution.py:101
  19.8 1.7 fusion.34
  21.5 3.1 %all-gather.1 = bf16[2,222,512]{2,1,0:T(8,128)(2,1)S(1)} all-gather(bf16[1,222,512]{2,1,0:T(8,128)(2,1)S(1)} %fusion.34), channel_id=1, replica_groups=mesh['scene'=2,'seq'=4,'head'=2,'band'=2] {'band'}, dimensions={0}, use_global_device_ids=true | all-gather | bytes 681984 | tf_op jit(solution)/shard_map/all_gather | solution.py:125
  27.0 1.6 fusion.33
  28.7 2.1 %all-gather = bf16[2,222,512]{2,1,0:T(8,128)(2,1)S(1)} all-gather(bf16[1,222,512]{2,1,0:T(8,128)(2,1)S(1)} %fusion.33), channel_id=1, replica_groups=mesh['scene'=2,'seq'=4,'head'=2,'band'=2] {'band'}, dimensions={0}, use_global_device_ids=true | all-gather | bytes 681984 | tf_op jit(solution)/shard_map/all_gather | solution.py:126
  34.8 3.4 %all-to-all-start = ((bf16[2,111,512]{2,1,0:T(8,128)(2,1)}), bf16[2,111,512]{2,1,0:T(8,128)(2,1)S(1)}, u32[]{:S(2)}, u32[]{:S(2)}) async-start(bf16[2,111,512]{2,1,0:T(8,128)(2,1)} %copy.47), calls=%async_computation | async-start | bytes 458752 | tf_op jit(solution)/shard_map/all_to_all | solution.py:130
  38.5 7.6 %all-to-all-done = bf16[2,111,512]{2,1,0:T(8,128)(2,1)S(1)} async-done(((bf16[2,111,512]{2,1,0:T(8,128)(2,1)}), bf16[2,111,512]{2,1,0:T(8,128)(2,1)S(1)}, u32[]{:S(2)}, u32[]{:S(2)}) %all-to-all-start) | async-done | bytes 227360 | tf_op jit(solution)/shard_map/all_to_all | solution.py:130
  47.0 2.1 %convert_reduce_fusion.1 = (f32[111]{0:T(128)S(1)}, bf16[111,1024]{1,0:T(8,128)(2,1)S(1)}) fusion(f32[111,1024]{1,0:T(8,128)S(1)} %reshape.316, bf16[111,1024]{1,0:T(8,128)(2,1)S(1)} %bitcast.210, bf16[1024,1024]{1,0:T(8,128)(2,1)} %all-gather.9.cloned.1.call-done), kind=kOutput, calls=%fused_computation.81 | convolution fusion | flops 233238416 | bytes 3006908 | tf_op jit(solution)/shard_map/dot_general | solution.py:131
  49.8 7.3 %all_gather.28 = bf16[1,6,37,1024]{3,2,0,1:T(8,128)(2,1)S(1)} all-gather(bf16[1,3,37,1024]{3,2,0,1:T(8,128)(2,1)S(1)} %multiply_convert_fusion), channel_id=1, replica_groups=mesh['scene'=2,'seq'=4,'head'=2,'band'=2] {'head'}, dimensions={1}, use_global_device_ids=true | all-gather | bytes 681984 | tf_op jit(solution)/shard_map/all_gather | solution.py:101
  57.3 2.3 %fusion.35 = bf16[1,222,512]{2,1,0:T(8,128)(2,1)} fusion(bf16[222,1024]{1,0:T(8,128)(2,1)S(1)} %reshape.321, bf16[3,1024,512]{2,1,0:T(8,128)(2,1)} %param.18), kind=kOutput, calls=%fused_computation.41 | convolution fusion | flops 232897536 | bytes 1730560 | tf_op jit(solution)/shard_map/dot_general | solution.py:106
  59.7 2.3 %fusion.36 = bf16[1,222,512]{2,1,0:T(8,128)(2,1)} fusion(bf16[222,1024]{1,0:T(8,128)(2,1)S(1)} %reshape.321, bf16[3,1024,512]{2,1,0:T(8,128)(2,1)} %param.18), kind=kOutput, calls=%fused_computation.42 | convolution fusion | flops 232897536 | bytes 1730560 | tf_op jit(solution)/shard_map/dot_general | solution.py:109
  62.7 1.6 convolution_convert_fusion.1
  65.2 23.2 %all-gather.13.cloned.1.call-done = bf16[8,222,512]{2,1,0:T(8,128)(2,1)} async-done(((bf16[1,222,512]{2,1,0:T(8,128)(2,1)}), bf16[8,222,512]{2,1,0:T(8,128)(2,1)}) %all-gather.13.cloned.1.call-update) | async-done | bytes 1818640 | tf_op jit(solution)/shard_map/all_gather | solution.py:117
  88.3 2.7 %reshape.322 = bf16[2,888,512]{2,1,0:T(8,128)(2,1)} reshape(bf16[8,222,512]{2,1,0:T(8,128)(2,1)} %all-gather.13.cloned.1.call-done) | data formatting | bytes 3637248 | tf_op jit(solution)/shard_map/reshape | solution.py:75
  91.1 25.4 %all-gather.15.cloned.1.call-done = bf16[8,222,512]{2,1,0:T(8,128)(2,1)} async-done(((bf16[1,222,512]{2,1,0:T(8,128)(2,1)}), bf16[8,222,512]{2,1,0:T(8,128)(2,1)}) %all-gather.15.cloned.1.call-update) | async-done | bytes 1818640 | tf_op jit(solution)/shard_map/all_gather | solution.py:118
  116.4 2.6 %reshape.324 = bf16[2,888,512]{2,1,0:T(8,128)(2,1)} reshape(bf16[8,222,512]{2,1,0:T(8,128)(2,1)} %all-gather.15.cloned.1.call-done) | data formatting | bytes 3637248 | tf_op jit(solution)/shard_map/reshape | solution.py:76
  119.1 36.0 %while.15 = (s32[]{:T(128)}, f32[222,8]{0,1:T(8,128)S(1)}, f32[222,8]{0,1:T(8,128)S(1)}, f32[222,8,64]{0,2,1:T(8,128)S(1)}, bf16[2,888,512]{2,1,0:T(8,128)(2,1)}...) while((s32[]{:T(128)}, f32[222,8]{0,1:T(8,128)S(1)}, ...), condition=%wide.region_9.10_spmd.clone, body=%wide.region_6.9_spmd.clone.sunk | while | flops 416701120 | bytes 29268588 | solution.py:95
  119.1 2.5 %constant_dynamic-slice_fusion.3 = (bf16[1,888,512]{2,1,0:T(8,128)(2,1)S(1)}, bf16[1,888,512]{2,1,0:T(8,128)(2,1)}) fusion(bf16[2,888,512]{2,1,0:T(8,128)(2,1)} %get-tuple-element.201, s32[]{:T(128)} %get-tuple-element.186, bf16[2,888,512]{2,1,0:T(8,128)(2,1)} %get-tuple-element.199), kind=kLoop, calls=%fused_computation.15.clone.1 | loop fusion | bytes 3637252 | tf_op jit(solution)/shard_map/while/body/jit(dynamic_index_in_dim)/dynamic_slice | solution.py:95
  123.1 4.7 %bitcast_reduce_fusion.3 = (f32[222,8]{0,1:T(8,128)S(1)}, f32[8,888,222]{1,2,0:T(8,128)}) fusion(bf16[888,8,64]{0,2,1:T(8,128)(2,1)S(1)} %bitcast.207, bf16[222,8,64]{0,2,1:T(8,128)(2,1)} %get-tuple-element.200), kind=kOutput, calls=%fused_computation.1.clone.1 | convolution fusion | flops 205019664 | bytes 7452096 | tf_op jit(solution)/shard_map/while/body/eval_jaxpr/qhd,khd->qhk/dot_general | solution.py:80
  127.9 4.1 %fusion.127 = f32[222,8]{0,1:T(8,128)S(1)} fusion(f32[8,888,222]{1,2,0:T(8,128)} %get-tuple-element.173, f32[222,8]{0,1:T(8,128)S(1)} %select_maximum_fusion.2), kind=kLoop, calls=%fused_computation.4.clone.1 | loop fusion | flops 4729488 | bytes 6322560 | tf_op jit(solution)/shard_map/while/body/eval_jaxpr/reduce_sum | solution.py:86
  132.6 4.4 %fusion.129 = f32[222,8,64]{0,2,1:T(8,128)S(1)} fusion(bf16[888,8,64]{0,2,1:T(8,128)(2,1)S(1)} %bitcast.206, f32[8,888,222]{1,2,0:T(8,128)} %get-tuple-element.173, f32[222,8]{0,1:T(8,128)S(1)} %select_maximum_fusion.2, f32[222,8,64]{0,2,1:T(8,128)S(1)} %get-tuple-element.189, f32[222,8]{0,1:T(8,128)S(1)} %get-tuple-element.176, pred[]{:T(512)S(6)} %compare.44), kind=kOutput, calls=%fused_computation.9.clone.1 | convolution fusion | flops 206939520 | bytes 8141185 | tf_op jit(solution)/shard_map/while/body/eval_jaxpr/qhk,khd->qhd/dot_general | solution.py:87
  137.1 2.5 %constant_dynamic-slice_fusion.3 = (bf16[1,888,512]{2,1,0:T(8,128)(2,1)S(1)}, bf16[1,888,512]{2,1,0:T(8,128)(2,1)}) fusion(bf16[2,888,512]{2,1,0:T(8,128)(2,1)} %get-tuple-element.201, s32[]{:T(128)} %get-tuple-element.186, bf16[2,888,512]{2,1,0:T(8,128)(2,1)} %get-tuple-element.199), kind=kLoop, calls=%fused_computation.15.clone.1 | loop fusion | bytes 3637252 | tf_op jit(solution)/shard_map/while/body/jit(dynamic_index_in_dim)/dynamic_slice | solution.py:95
  141.1 4.7 %bitcast_reduce_fusion.3 = (f32[222,8]{0,1:T(8,128)S(1)}, f32[8,888,222]{1,2,0:T(8,128)}) fusion(bf16[888,8,64]{0,2,1:T(8,128)(2,1)S(1)} %bitcast.207, bf16[222,8,64]{0,2,1:T(8,128)(2,1)} %get-tuple-element.200), kind=kOutput, calls=%fused_computation.1.clone.1 | convolution fusion | flops 205019664 | bytes 7452096 | tf_op jit(solution)/shard_map/while/body/eval_jaxpr/qhd,khd->qhk/dot_general | solution.py:80
  145.8 4.1 %fusion.127 = f32[222,8]{0,1:T(8,128)S(1)} fusion(f32[8,888,222]{1,2,0:T(8,128)} %get-tuple-element.173, f32[222,8]{0,1:T(8,128)S(1)} %select_maximum_fusion.2), kind=kLoop, calls=%fused_computation.4.clone.1 | loop fusion | flops 4729488 | bytes 6322560 | tf_op jit(solution)/shard_map/while/body/eval_jaxpr/reduce_sum | solution.py:86
  150.6 4.4 %fusion.129 = f32[222,8,64]{0,2,1:T(8,128)S(1)} fusion(bf16[888,8,64]{0,2,1:T(8,128)(2,1)S(1)} %bitcast.206, f32[8,888,222]{1,2,0:T(8,128)} %get-tuple-element.173, f32[222,8]{0,1:T(8,128)S(1)} %select_maximum_fusion.2, f32[222,8,64]{0,2,1:T(8,128)S(1)} %get-tuple-element.189, f32[222,8]{0,1:T(8,128)S(1)} %get-tuple-element.176, pred[]{:T(512)S(6)} %compare.44), kind=kOutput, calls=%fused_computation.9.clone.1 | convolution fusion | flops 206939520 | bytes 8141185 | tf_op jit(solution)/shard_map/while/body/eval_jaxpr/qhk,khd->qhd/dot_general | solution.py:87
  156.2 3.6 %all-to-all-start.1 = ((bf16[2,111,512]{2,1,0:T(8,128)(2,1)}), bf16[2,111,512]{2,1,0:T(8,128)(2,1)S(1)}, u32[]{:S(2)}, u32[]{:S(2)}) async-start(bf16[2,111,512]{2,1,0:T(8,128)(2,1)} %copy.53), calls=%async_computation.1 | async-start | bytes 458752 | tf_op jit(solution)/shard_map/all_to_all | solution.py:130
  159.8 1.8 convert_element_type.136
  161.5 2.8 %all-to-all-done.1 = bf16[2,111,512]{2,1,0:T(8,128)(2,1)S(1)} async-done(((bf16[2,111,512]{2,1,0:T(8,128)(2,1)}), bf16[2,111,512]{2,1,0:T(8,128)(2,1)S(1)}, u32[]{:S(2)}, u32[]{:S(2)}) %all-to-all-start.1) | async-done | bytes 227360 | tf_op jit(solution)/shard_map/all_to_all | solution.py:130
  164.9 2.9 %fusion.97 = (f32[111,1024]{1,0:T(8,128)}, bf16[111,1024]{1,0:T(8,128)(2,1)S(1)}) fusion(bf16[111,1024]{1,0:T(8,128)(2,1)S(1)} %bitcast.211, bf16[1024,1024]{1,0:T(8,128)(2,1)} %all-gather.11.cloned.1.call-done, bf16[111,1024]{1,0:T(8,128)(2,1)S(1)} %copy-done.2), kind=kOutput, calls=%fused_computation.135 | convolution fusion | flops 233238528 | bytes 3233792 | tf_op jit(solution)/shard_map/dot_general | solution.py:131
  170.0 3.0 %collective-permute-start = (bf16[1,1,37,256]{3,2,1,0:T(8,128)(2,1)S(1)}, bf16[1,1,37,256]{3,2,1,0:T(8,128)(2,1)S(1)}, u32[]{:S(2)}, u32[]{:S(2)}) collective-permute-start(bf16[1,1,37,256]{3,2,1,0:T(8,128)(2,1)S(1)} %get-tuple-element.114), channel_id=1, source_target_pairs={{0,1},{1,2},{2,3},{4,5},{5,6},{6,7},{8,9},{9,10},{10,11},{12,13},{... | collective-permute-start | bytes 56840 | tf_op jit(solution)/shard_map/ppermute | solution.py:16
  173.0 1.9 %collective-permute-start.1 = (bf16[1,1,37,256]{3,2,1,0:T(8,128)(2,1)S(1)}, bf16[1,1,37,256]{3,2,1,0:T(8,128)(2,1)S(1)}, u32[]{:S(2)}, u32[]{:S(2)}) collective-permute-start(bf16[1,1,37,256]{3,2,1,0:T(8,128)(2,1)S(1)} %get-tuple-element.115), channel_id=1, source_target_pairs={{1,0},{2,1},{3,2},{5,4},{6,5},{7,6},{9,8},{10,9},{11,10},{13,12},{... | collective-permute-start | bytes 56840 | tf_op jit(solution)/shard_map/ppermute | solution.py:19
  175.0 3.1 %collective-permute-done.1 = bf16[1,1,37,256]{3,2,1,0:T(8,128)(2,1)S(1)} collective-permute-done((bf16[1,1,37,256]{3,2,1,0:T(8,128)(2,1)S(1)}, bf16[1,1,37,256]{3,2,1,0:T(8,128)(2,1)S(1)}, u32[]{:S(2)}, u32[]{:S(2)}) %collective-permute-start.1) | collective-permute-done | bytes 18976 | tf_op jit(solution)/shard_map/ppermute | solution.py:19
  (104 shorter events, 24.4 us)
Async XLA Ops:
  7.2 161.3 %copy-start = (bf16[2048,256]{1,0:T(8,128)(2,1)S(1)}, bf16[2048,256]{1,0:T(8,128)(2,1)}, u32[]{:S(2)}) copy-start(bf16[2048,256]{1,0:T(8,128)(2,1)} %param.21) | copy-start | bytes 3145732
  7.2 39.8 %all-gather.9.cloned.1.call-start = ((), (), s32[]{:S(2)}) async-start(), calls=%async_computation.2 | async-start | bytes 3145728 | tf_op jit(solution)/shard_map/all_gather | solution.py:133
  33.0 5.4 %copy-start.3 = (bf16[1,3,37,1024]{3,2,1,0:T(8,128)(2,1)S(1)}, bf16[1,3,37,1024]{3,2,1,0:T(8,128)(2,1)}, u32[]{:S(2)}) copy-start(bf16[1,3,37,1024]{3,2,1,0:T(8,128)(2,1)} %param.13) | copy-start | bytes 681988
  34.8 11.3 %all-to-all-start = ((bf16[2,111,512]{2,1,0:T(8,128)(2,1)}), bf16[2,111,512]{2,1,0:T(8,128)(2,1)S(1)}, u32[]{:S(2)}, u32[]{:S(2)}) async-start(bf16[2,111,512]{2,1,0:T(8,128)(2,1)} %copy.47), calls=%async_computation | async-start | bytes 458752 | tf_op jit(solution)/shard_map/all_to_all | solution.py:130
  38.3 50.1 %all-gather.13.cloned.1.call-start = ((), (), s32[]{:S(2)}) async-start(), calls=%async_computation.4 | async-start | bytes 2064384 | tf_op jit(solution)/shard_map/all_gather | solution.py:117
  38.4 11.3 %copy-start.8 = (f32[1024]{0:T(1024)S(1)}, f32[1024]{0:T(1024)}, u32[]{:S(2)}) copy-start(f32[1024]{0:T(1024)} %param.17) | copy-start | bytes 12292
  49.2 12.9 %copy-start.1 = (bf16[111,1024]{1,0:T(8,128)(2,1)}, bf16[111,1024]{1,0:T(8,128)(2,1)S(1)}, u32[]{:S(2)}) copy-start(bf16[111,1024]{1,0:T(8,128)(2,1)S(1)} %get-tuple-element.119) | copy-start | bytes 681988
  49.3 12.8 %copy-start.4 = (bf16[1,3,37,1024]{3,2,1,0:T(8,128)(2,1)}, bf16[1,3,37,1024]{3,2,1,0:T(8,128)(2,1)S(1)}, u32[]{:S(2)}) copy-start(bf16[1,3,37,1024]{3,2,1,0:T(8,128)(2,1)S(1)} %convert_element_type.137) | copy-start | bytes 681988
  59.7 56.8 %all-gather.15.cloned.1.call-start = ((), (), s32[]{:S(2)}) async-start(), calls=%async_computation.5 | async-start | bytes 2064384 | tf_op jit(solution)/shard_map/all_gather | solution.py:118
  62.1 102.7 %all-gather.11.cloned.1.call-start = ((), (), s32[]{:S(2)}) async-start(), calls=%async_computation.3 | async-start | bytes 3145728 | tf_op jit(solution)/shard_map/all_gather | solution.py:133
  155.0 9.8 %copy-start.2 = (bf16[111,1024]{1,0:T(8,128)(2,1)S(1)}, bf16[111,1024]{1,0:T(8,128)(2,1)}, u32[]{:S(2)}) copy-start(bf16[111,1024]{1,0:T(8,128)(2,1)} %copy-done.1) | copy-start | bytes 681988
  156.2 11.9 %copy-start.5 = (bf16[1,3,37,1024]{3,2,1,0:T(8,128)(2,1)S(1)}, bf16[1,3,37,1024]{3,2,1,0:T(8,128)(2,1)}, u32[]{:S(2)}) copy-start(bf16[1,3,37,1024]{3,2,1,0:T(8,128)(2,1)} %copy-done.4) | copy-start | bytes 681988
  156.2 8.2 %all-to-all-start.1 = ((bf16[2,111,512]{2,1,0:T(8,128)(2,1)}), bf16[2,111,512]{2,1,0:T(8,128)(2,1)S(1)}, u32[]{:S(2)}, u32[]{:S(2)}) async-start(bf16[2,111,512]{2,1,0:T(8,128)(2,1)} %copy.53), calls=%async_computation.1 | async-start | bytes 458752 | tf_op jit(solution)/shard_map/all_to_all | solution.py:130
  159.7 8.7 %copy-start.9 = (f32[2048]{0:T(1024)S(1)}, f32[2048]{0:T(1024)}, u32[]{:S(2)}) copy-start(f32[2048]{0:T(1024)} %param.20) | copy-start | bytes 24580
  159.8 8.7 %copy-start.10 = (f32[256]{0:T(256)S(1)}, f32[256]{0:T(256)}, u32[]{:S(2)}) copy-start(f32[256]{0:T(256)} %param.22) | copy-start | bytes 3076
  164.8 13.3 %copy-start.6 = (bf16[3,3,256,256]{3,2,1,0:T(8,128)(2,1)S(1)}, bf16[3,3,256,256]{3,2,1,0:T(8,128)(2,1)}, u32[]{:S(2)}) copy-start(bf16[3,3,256,256]{3,2,1,0:T(8,128)(2,1)} %param.23) | copy-start | bytes 3538948
  168.0 11.6 %copy-start.7 = (bf16[1,3,37,1024]{3,2,1,0:T(8,128)(2,1)}, bf16[1,3,37,1024]{3,2,1,0:T(8,128)(2,1)S(1)}, u32[]{:S(2)}) copy-start(bf16[1,3,37,1024]{3,2,1,0:T(8,128)(2,1)S(1)} %reshape.325) | copy-start | bytes 681988
  170.0 4.9 %collective-permute-start = (bf16[1,1,37,256]{3,2,1,0:T(8,128)(2,1)S(1)}, bf16[1,1,37,256]{3,2,1,0:T(8,128)(2,1)S(1)}, u32[]{:S(2)}, u32[]{:S(2)}) collective-permute-start(bf16[1,1,37,256]{3,2,1,0:T(8,128)(2,1)S(1)} %get-tuple-element.114), channel_id=1, source_target_pairs={{0,1},{1,2},{2,3},{4,5},{5,6},{6,7},{8,9},{9,10},{10,11},{12,13},{... | collective-permute-start | bytes 56840 | tf_op jit(solution)/shard_map/ppermute | solution.py:16
  173.0 5.1 %collective-permute-start.1 = (bf16[1,1,37,256]{3,2,1,0:T(8,128)(2,1)S(1)}, bf16[1,1,37,256]{3,2,1,0:T(8,128)(2,1)S(1)}, u32[]{:S(2)}, u32[]{:S(2)}) collective-permute-start(bf16[1,1,37,256]{3,2,1,0:T(8,128)(2,1)S(1)} %get-tuple-element.115), channel_id=1, source_target_pairs={{1,0},{2,1},{3,2},{5,4},{6,5},{7,6},{9,8},{10,9},{11,10},{13,12},{... | collective-permute-start | bytes 56840 | tf_op jit(solution)/shard_map/ppermute | solution.py:19
Sparse Core Ops, SparseCore 0:
  9.5 37.4 all-gather.8
  59.8 28.5 all-gather.12
  90.0 26.3 all-gather.14
  117.8 31.9 all-gather.10
where the time goes:
time: 188 us; the launch traced here: 187 us
  waiting for transfers between devices  63.7 us (34%)
  matrix products  39.8 us (21%)
  local copies, waits for them, and re-layouts  21 us (11%)
  blocking collectives  20.9 us (11%)
  other arithmetic  15 us (8%)
  between operations  14.2 us (8%)
  starting transfers between devices  12.2 us (6%)
    all_gather x1, waiting for transfers between devices, attention_block(): lax.all_gather(value_rows, ('seq', 'band'), axis=0, tiled=True)  25.4 us
    all_gather x1, waiting for transfers between devices, attention_block(): lax.all_gather(key_rows, ('seq', 'band'), axis=0, tiled=True)  23.2 us
    all_gather x2, blocking collectives, attention_block(): gathered = lax.all_gather(normed, 'head', axis=1, tiled=True)  15.7 us
    all_to_all x2, waiting for transfers between devices, attention_block(): lax.all_to_all(attended, 'head', split_axis=0, concat_axis=1, tiled=True)  10.5 us
    dot_general x2, matrix products, absorb(): jnp.einsum('qhd,khd->qhk', heads_q, by_heads(blocks_pair[0]), preferred_e...  9.42 us
    dynamic_slice x6, local copies, waits for them, and re-layouts, fold_keys(): carry, ignored = lax.scan(absorb, carry, (key_blocks, value_blocks))  9.3 us
    dot_general x2, matrix products, absorb(): jnp.einsum('qhk,khd->qhd', probs.astype(jnp.bfloat16), by_heads(blocks_pa...  8.89 us
    reduce_sum x2, other arithmetic, absorb(): running_sum = running_sum * decay + jnp.sum(probs, axis=-1)  8.21 us
  transfers between devices with their start and end apart: 8, of which 6 were waited for; matrix products, arithmetic and copies ran while one was open for 34% of the time, Pallas kernels for 0%

commit v1 on v0

--- a/solution.py
+++ b/solution.py
@@ -127,7 +127,10 @@
         )
         attended = attend_local(query_rows, keys_all, values_all)
     band_rows = inputs.shape[1] * inputs.shape[2]
-    own_rows = lax.all_to_all(attended, "head", split_axis=0, concat_axis=1, tiled=True)
+    n_dev = lax.axis_size("head")
+    parts = jnp.stack(jnp.split(attended, n_dev, axis=0), axis=0)
+    parts = lax.all_to_all(parts, "head", split_axis=0, concat_axis=0)
+    own_rows = jnp.concatenate(parts, axis=1)
     branch = jnp.dot(
         own_rows,
         lax.all_gather(out_weight, "head", axis=0, tiled=True),

time: 188 us -> 188 us (level)
    convert_element_type x4 -> x0, local copies, waits for them, and re-layouts: 2.11 us -> none  [the longest x2 1.06 us: attend_local(): return mixed.reshape(queries.shape).astype(jnp.bfloat16)]
where the time goes in v1:
time: 188 us; the launch traced here: 187 us
  waiting for transfers between devices  63.7 us (34%)
  matrix products  39.8 us (21%)
  blocking collectives  20.9 us (11%)
  local copies, waits for them, and re-layouts  20.2 us (11%)
  other arithmetic  15.8 us (8%)
  between operations  14.2 us (8%)
  starting transfers between devices  12.2 us (6%)
    all_gather x1, waiting for transfers between devices, attention_block(): lax.all_gather(value_rows, ('seq', 'band'), axis=0, tiled=True)  25.4 us
    all_gather x1, waiting for transfers between devices, attention_block(): lax.all_gather(key_rows, ('seq', 'band'), axis=0, tiled=True)  23.2 us
    all_gather x2, blocking collectives, attention_block(): gathered = lax.all_gather(normed, 'head', axis=1, tiled=True)  15.7 us
    all_to_all x2, waiting for transfers between devices, attention_block(): parts = lax.all_to_all(parts, 'head', split_axis=0, concat_axis=0)  10.5 us
    dot_general x2, matrix products, absorb(): jnp.einsum('qhd,khd->qhk', heads_q, by_heads(blocks_pair[0]), preferred_e...  9.44 us
    dynamic_slice x6, local copies, waits for them, and re-layouts, fold_keys(): carry, ignored = lax.scan(absorb, carry, (key_blocks, value_blocks))  9.28 us
    dot_general x2, matrix products, absorb(): jnp.einsum('qhk,khd->qhd', probs.astype(jnp.bfloat16), by_heads(blocks_pa...  8.89 us
    reduce_sum x2, other arithmetic, absorb(): running_sum = running_sum * decay + jnp.sum(probs, axis=-1)  8.21 us
  transfers between devices with their start and end apart: 8, of which 6 were waited for; matrix products, arithmetic and copies ran while one was open for 34% of the time, Pallas kernels for 0%

profile of v1, /device:TPU:1, one launch (start us, length us, event | category | flops | bytes accessed | tf_op | source)
XLA Modules:
  0.0 186.9 jit_solution(16472195319417803567)
XLA Ops:
  11.3 8.4 %all_gather.24 = bf16[1,6,37,1024]{3,2,0,1:T(8,128)(2,1)S(1)} all-gather(bf16[1,3,37,1024]{3,2,0,1:T(8,128)(2,1)S(1)} %multiply_convert_fusion.1), channel_id=1, replica_groups=mesh['scene'=2,'seq'=4,'head'=2,'band'=2] {'head'}, dimensions={1}, use_global_device_ids=true | all-gather | bytes 681984 | tf_op jit(solution)/shard_map/all_gather | solution.py:101
  19.8 1.7 fusion.34
  21.5 3.1 %all-gather.1 = bf16[2,222,512]{2,1,0:T(8,128)(2,1)S(1)} all-gather(bf16[1,222,512]{2,1,0:T(8,128)(2,1)S(1)} %fusion.34), channel_id=1, replica_groups=mesh['scene'=2,'seq'=4,'head'=2,'band'=2] {'band'}, dimensions={0}, use_global_device_ids=true | all-gather | bytes 681984 | tf_op jit(solution)/shard_map/all_gather | solution.py:125
  27.0 1.6 fusion.33
  28.7 2.1 %all-gather = bf16[2,222,512]{2,1,0:T(8,128)(2,1)S(1)} all-gather(bf16[1,222,512]{2,1,0:T(8,128)(2,1)S(1)} %fusion.33), channel_id=1, replica_groups=mesh['scene'=2,'seq'=4,'head'=2,'band'=2] {'band'}, dimensions={0}, use_global_device_ids=true | all-gather | bytes 681984 | tf_op jit(solution)/shard_map/all_gather | solution.py:126
  34.9 3.4 %all-to-all-start = ((bf16[2,111,512]{2,1,0:T(8,128)(2,1)}), bf16[2,111,512]{2,1,0:T(8,128)(2,1)S(1)}, u32[]{:S(2)}, u32[]{:S(2)}) async-start(bf16[2,111,512]{2,1,0:T(8,128)(2,1)} %pad_maximum_fusion.1), calls=%async_computation | async-start | bytes 458752 | tf_op jit(solution)/shard_map/all_to_all | solution.py:132
  38.5 7.6 %all-to-all-done = bf16[2,111,512]{2,1,0:T(8,128)(2,1)S(1)} async-done(((bf16[2,111,512]{2,1,0:T(8,128)(2,1)}), bf16[2,111,512]{2,1,0:T(8,128)(2,1)S(1)}, u32[]{:S(2)}, u32[]{:S(2)}) %all-to-all-start) | async-done | bytes 227360 | tf_op jit(solution)/shard_map/all_to_all | solution.py:132
  47.0 2.1 %convert_reduce_fusion.1 = (f32[111]{0:T(128)S(1)}, bf16[111,1024]{1,0:T(8,128)(2,1)S(1)}) fusion(f32[111,1024]{1,0:T(8,128)S(1)} %reshape.328, bf16[111,1024]{1,0:T(8,128)(2,1)S(1)} %bitcast.210, bf16[1024,1024]{1,0:T(8,128)(2,1)} %all-gather.9.cloned.1.call-done), kind=kOutput, calls=%fused_computation.81 | convolution fusion | flops 233238416 | bytes 3006908 | tf_op jit(solution)/shard_map/dot_general | solution.py:134
  49.8 7.3 %all_gather.28 = bf16[1,6,37,1024]{3,2,0,1:T(8,128)(2,1)S(1)} all-gather(bf16[1,3,37,1024]{3,2,0,1:T(8,128)(2,1)S(1)} %multiply_convert_fusion), channel_id=1, replica_groups=mesh['scene'=2,'seq'=4,'head'=2,'band'=2] {'head'}, dimensions={1}, use_global_device_ids=true | all-gather | bytes 681984 | tf_op jit(solution)/shard_map/all_gather | solution.py:101
  57.3 2.3 %fusion.35 = bf16[1,222,512]{2,1,0:T(8,128)(2,1)} fusion(bf16[222,1024]{1,0:T(8,128)(2,1)S(1)} %reshape.335, bf16[3,1024,512]{2,1,0:T(8,128)(2,1)} %param.18), kind=kOutput, calls=%fused_computation.41 | convolution fusion | flops 232897536 | bytes 1730560 | tf_op jit(solution)/shard_map/dot_general | solution.py:106
  59.7 2.3 %fusion.36 = bf16[1,222,512]{2,1,0:T(8,128)(2,1)} fusion(bf16[222,1024]{1,0:T(8,128)(2,1)S(1)} %reshape.335, bf16[3,1024,512]{2,1,0:T(8,128)(2,1)} %param.18), kind=kOutput, calls=%fused_computation.42 | convolution fusion | flops 232897536 | bytes 1730560 | tf_op jit(solution)/shard_map/dot_general | solution.py:109
  62.7 1.6 convolution_convert_fusion.1
  65.2 23.2 %all-gather.13.cloned.1.call-done = bf16[8,222,512]{2,1,0:T(8,128)(2,1)} async-done(((bf16[1,222,512]{2,1,0:T(8,128)(2,1)}), bf16[8,222,512]{2,1,0:T(8,128)(2,1)}) %all-gather.13.cloned.1.call-update) | async-done | bytes 1818640 | tf_op jit(solution)/shard_map/all_gather | solution.py:117
  88.4 2.7 %reshape.336 = bf16[2,888,512]{2,1,0:T(8,128)(2,1)} reshape(bf16[8,222,512]{2,1,0:T(8,128)(2,1)} %all-gather.13.cloned.1.call-done) | data formatting | bytes 3637248 | tf_op jit(solution)/shard_map/reshape | solution.py:75
  91.1 25.4 %all-gather.15.cloned.1.call-done = bf16[8,222,512]{2,1,0:T(8,128)(2,1)} async-done(((bf16[1,222,512]{2,1,0:T(8,128)(2,1)}), bf16[8,222,512]{2,1,0:T(8,128)(2,1)}) %all-gather.15.cloned.1.call-update) | async-done | bytes 1818640 | tf_op jit(solution)/shard_map/all_gather | solution.py:118
  116.5 2.6 %reshape.338 = bf16[2,888,512]{2,1,0:T(8,128)(2,1)} reshape(bf16[8,222,512]{2,1,0:T(8,128)(2,1)} %all-gather.15.cloned.1.call-done) | data formatting | bytes 3637248 | tf_op jit(solution)/shard_map/reshape | solution.py:76
  119.1 36.0 %while.15 = (s32[]{:T(128)}, f32[222,8]{0,1:T(8,128)S(1)}, f32[222,8]{0,1:T(8,128)S(1)}, f32[222,8,64]{0,2,1:T(8,128)S(1)}, bf16[2,888,512]{2,1,0:T(8,128)(2,1)}...) while((s32[]{:T(128)}, f32[222,8]{0,1:T(8,128)S(1)}, ...), condition=%wide.region_9.10_spmd.clone, body=%wide.region_6.9_spmd.clone.sunk | while | flops 416701120 | bytes 29268588 | solution.py:95
  119.1 2.5 %constant_dynamic-slice_fusion.3 = (bf16[1,888,512]{2,1,0:T(8,128)(2,1)S(1)}, bf16[1,888,512]{2,1,0:T(8,128)(2,1)}) fusion(bf16[2,888,512]{2,1,0:T(8,128)(2,1)} %get-tuple-element.205, s32[]{:T(128)} %get-tuple-element.190, bf16[2,888,512]{2,1,0:T(8,128)(2,1)} %get-tuple-element.203), kind=kLoop, calls=%fused_computation.15.clone.1 | loop fusion | bytes 3637252 | tf_op jit(solution)/shard_map/while/body/jit(dynamic_index_in_dim)/dynamic_slice | solution.py:95
  123.2 4.7 %bitcast_reduce_fusion.3 = (f32[222,8]{0,1:T(8,128)S(1)}, f32[8,888,222]{1,2,0:T(8,128)}) fusion(bf16[888,8,64]{0,2,1:T(8,128)(2,1)S(1)} %bitcast.207, bf16[222,8,64]{0,2,1:T(8,128)(2,1)} %get-tuple-element.204), kind=kOutput, calls=%fused_computation.1.clone.1 | convolution fusion | flops 205019664 | bytes 7452096 | tf_op jit(solution)/shard_map/while/body/eval_jaxpr/qhd,khd->qhk/dot_general | solution.py:80
  127.9 4.1 %fusion.129 = f32[222,8]{0,1:T(8,128)S(1)} fusion(f32[8,888,222]{1,2,0:T(8,128)} %get-tuple-element.177, f32[222,8]{0,1:T(8,128)S(1)} %select_maximum_fusion.2), kind=kLoop, calls=%fused_computation.4.clone.1 | loop fusion | flops 4729488 | bytes 6322560 | tf_op jit(solution)/shard_map/while/body/eval_jaxpr/reduce_sum | solution.py:86
  132.6 4.4 %fusion.131 = f32[222,8,64]{0,2,1:T(8,128)S(1)} fusion(bf16[888,8,64]{0,2,1:T(8,128)(2,1)S(1)} %bitcast.206, f32[8,888,222]{1,2,0:T(8,128)} %get-tuple-element.177, f32[222,8]{0,1:T(8,128)S(1)} %select_maximum_fusion.2, f32[222,8,64]{0,2,1:T(8,128)S(1)} %get-tuple-element.193, f32[222,8]{0,1:T(8,128)S(1)} %get-tuple-element.180, pred[]{:T(512)S(6)} %compare.44), kind=kOutput, calls=%fused_computation.9.clone.1 | convolution fusion | flops 206939520 | bytes 8141185 | tf_op jit(solution)/shard_map/while/body/eval_jaxpr/qhk,khd->qhd/dot_general | solution.py:87
  137.1 2.5 %constant_dynamic-slice_fusion.3 = (bf16[1,888,512]{2,1,0:T(8,128)(2,1)S(1)}, bf16[1,888,512]{2,1,0:T(8,128)(2,1)}) fusion(bf16[2,888,512]{2,1,0:T(8,128)(2,1)} %get-tuple-element.205, s32[]{:T(128)} %get-tuple-element.190, bf16[2,888,512]{2,1,0:T(8,128)(2,1)} %get-tuple-element.203), kind=kLoop, calls=%fused_computation.15.clone.1 | loop fusion | bytes 3637252 | tf_op jit(solution)/shard_map/while/body/jit(dynamic_index_in_dim)/dynamic_slice | solution.py:95
  141.1 4.7 %bitcast_reduce_fusion.3 = (f32[222,8]{0,1:T(8,128)S(1)}, f32[8,888,222]{1,2,0:T(8,128)}) fusion(bf16[888,8,64]{0,2,1:T(8,128)(2,1)S(1)} %bitcast.207, bf16[222,8,64]{0,2,1:T(8,128)(2,1)} %get-tuple-element.204), kind=kOutput, calls=%fused_computation.1.clone.1 | convolution fusion | flops 205019664 | bytes 7452096 | tf_op jit(solution)/shard_map/while/body/eval_jaxpr/qhd,khd->qhk/dot_general | solution.py:80
  145.9 4.1 %fusion.129 = f32[222,8]{0,1:T(8,128)S(1)} fusion(f32[8,888,222]{1,2,0:T(8,128)} %get-tuple-element.177, f32[222,8]{0,1:T(8,128)S(1)} %select_maximum_fusion.2), kind=kLoop, calls=%fused_computation.4.clone.1 | loop fusion | flops 4729488 | bytes 6322560 | tf_op jit(solution)/shard_map/while/body/eval_jaxpr/reduce_sum | solution.py:86
  150.6 4.4 %fusion.131 = f32[222,8,64]{0,2,1:T(8,128)S(1)} fusion(bf16[888,8,64]{0,2,1:T(8,128)(2,1)S(1)} %bitcast.206, f32[8,888,222]{1,2,0:T(8,128)} %get-tuple-element.177, f32[222,8]{0,1:T(8,128)S(1)} %select_maximum_fusion.2, f32[222,8,64]{0,2,1:T(8,128)S(1)} %get-tuple-element.193, f32[222,8]{0,1:T(8,128)S(1)} %get-tuple-element.180, pred[]{:T(512)S(6)} %compare.44), kind=kOutput, calls=%fused_computation.9.clone.1 | convolution fusion | flops 206939520 | bytes 8141185 | tf_op jit(solution)/shard_map/while/body/eval_jaxpr/qhk,khd->qhd/dot_general | solution.py:87
  156.2 3.6 %all-to-all-start.1 = ((bf16[2,111,512]{2,1,0:T(8,128)(2,1)}), bf16[2,111,512]{2,1,0:T(8,128)(2,1)S(1)}, u32[]{:S(2)}, u32[]{:S(2)}) async-start(bf16[2,111,512]{2,1,0:T(8,128)(2,1)} %copy.52), calls=%async_computation.1 | async-start | bytes 458752 | tf_op jit(solution)/shard_map/all_to_all | solution.py:132
  159.8 1.8 convert_element_type.129
  161.5 2.8 %all-to-all-done.1 = bf16[2,111,512]{2,1,0:T(8,128)(2,1)S(1)} async-done(((bf16[2,111,512]{2,1,0:T(8,128)(2,1)}), bf16[2,111,512]{2,1,0:T(8,128)(2,1)S(1)}, u32[]{:S(2)}, u32[]{:S(2)}) %all-to-all-start.1) | async-done | bytes 227360 | tf_op jit(solution)/shard_map/all_to_all | solution.py:132
  164.9 2.9 %fusion.99 = (f32[111,1024]{1,0:T(8,128)}, bf16[111,1024]{1,0:T(8,128)(2,1)S(1)}) fusion(bf16[111,1024]{1,0:T(8,128)(2,1)S(1)} %bitcast.211, bf16[1024,1024]{1,0:T(8,128)(2,1)} %all-gather.11.cloned.1.call-done, bf16[111,1024]{1,0:T(8,128)(2,1)S(1)} %copy-done.2), kind=kOutput, calls=%fused_computation.139 | convolution fusion | flops 233238528 | bytes 3233792 | tf_op jit(solution)/shard_map/dot_general | solution.py:134
  170.0 2.9 %collective-permute-start = (bf16[1,1,37,256]{3,2,1,0:T(8,128)(2,1)S(1)}, bf16[1,1,37,256]{3,2,1,0:T(8,128)(2,1)S(1)}, u32[]{:S(2)}, u32[]{:S(2)}) collective-permute-start(bf16[1,1,37,256]{3,2,1,0:T(8,128)(2,1)S(1)} %get-tuple-element.118), channel_id=1, source_target_pairs={{0,1},{1,2},{2,3},{4,5},{5,6},{6,7},{8,9},{9,10},{10,11},{12,13},{... | collective-permute-start | bytes 56840 | tf_op jit(solution)/shard_map/ppermute | solution.py:16
  173.0 1.9 %collective-permute-start.1 = (bf16[1,1,37,256]{3,2,1,0:T(8,128)(2,1)S(1)}, bf16[1,1,37,256]{3,2,1,0:T(8,128)(2,1)S(1)}, u32[]{:S(2)}, u32[]{:S(2)}) collective-permute-start(bf16[1,1,37,256]{3,2,1,0:T(8,128)(2,1)S(1)} %get-tuple-element.119), channel_id=1, source_target_pairs={{1,0},{2,1},{3,2},{5,4},{6,5},{7,6},{9,8},{10,9},{11,10},{13,12},{... | collective-permute-start | bytes 56840 | tf_op jit(solution)/shard_map/ppermute | solution.py:19
  175.0 3.1 %collective-permute-done.1 = bf16[1,1,37,256]{3,2,1,0:T(8,128)(2,1)S(1)} collective-permute-done((bf16[1,1,37,256]{3,2,1,0:T(8,128)(2,1)S(1)}, bf16[1,1,37,256]{3,2,1,0:T(8,128)(2,1)S(1)}, u32[]{:S(2)}, u32[]{:S(2)}) %collective-permute-start.1) | collective-permute-done | bytes 18976 | tf_op jit(solution)/shard_map/ppermute | solution.py:19
  (107 shorter events, 24.4 us)
Async XLA Ops:
  7.2 161.3 %copy-start = (bf16[2048,256]{1,0:T(8,128)(2,1)S(1)}, bf16[2048,256]{1,0:T(8,128)(2,1)}, u32[]{:S(2)}) copy-start(bf16[2048,256]{1,0:T(8,128)(2,1)} %param.21) | copy-start | bytes 3145732
  7.2 39.8 %all-gather.9.cloned.1.call-start = ((), (), s32[]{:S(2)}) async-start(), calls=%async_computation.2 | async-start | bytes 3145728 | tf_op jit(solution)/shard_map/all_gather | solution.py:136
  33.0 5.4 %copy-start.3 = (bf16[1,3,37,1024]{3,2,1,0:T(8,128)(2,1)S(1)}, bf16[1,3,37,1024]{3,2,1,0:T(8,128)(2,1)}, u32[]{:S(2)}) copy-start(bf16[1,3,37,1024]{3,2,1,0:T(8,128)(2,1)} %param.13) | copy-start | bytes 681988
  34.9 11.3 %all-to-all-start = ((bf16[2,111,512]{2,1,0:T(8,128)(2,1)}), bf16[2,111,512]{2,1,0:T(8,128)(2,1)S(1)}, u32[]{:S(2)}, u32[]{:S(2)}) async-start(bf16[2,111,512]{2,1,0:T(8,128)(2,1)} %pad_maximum_fusion.1), calls=%async_computation | async-start | bytes 458752 | tf_op jit(solution)/shard_map/all_to_all | solution.py:132
  38.3 50.1 %all-gather.13.cloned.1.call-start = ((), (), s32[]{:S(2)}) async-start(), calls=%async_computation.4 | async-start | bytes 2064384 | tf_op jit(solution)/shard_map/all_gather | solution.py:117
  38.4 11.2 %copy-start.8 = (f32[1024]{0:T(1024)S(1)}, f32[1024]{0:T(1024)}, u32[]{:S(2)}) copy-start(f32[1024]{0:T(1024)} %param.17) | copy-start | bytes 12292
  49.2 12.9 %copy-start.1 = (bf16[111,1024]{1,0:T(8,128)(2,1)}, bf16[111,1024]{1,0:T(8,128)(2,1)S(1)}, u32[]{:S(2)}) copy-start(bf16[111,1024]{1,0:T(8,128)(2,1)S(1)} %get-tuple-element.123) | copy-start | bytes 681988
  49.3 12.8 %copy-start.4 = (bf16[1,3,37,1024]{3,2,1,0:T(8,128)(2,1)}, bf16[1,3,37,1024]{3,2,1,0:T(8,128)(2,1)S(1)}, u32[]{:S(2)}) copy-start(bf16[1,3,37,1024]{3,2,1,0:T(8,128)(2,1)S(1)} %convert_element_type.130) | copy-start | bytes 681988
  59.7 56.8 %all-gather.15.cloned.1.call-start = ((), (), s32[]{:S(2)}) async-start(), calls=%async_computation.5 | async-start | bytes 2064384 | tf_op jit(solution)/shard_map/all_gather | solution.py:118
  62.1 102.8 %all-gather.11.cloned.1.call-start = ((), (), s32[]{:S(2)}) async-start(), calls=%async_computation.3 | async-start | bytes 3145728 | tf_op jit(solution)/shard_map/all_gather | solution.py:136
  155.1 9.8 %copy-start.2 = (bf16[111,1024]{1,0:T(8,128)(2,1)S(1)}, bf16[111,1024]{1,0:T(8,128)(2,1)}, u32[]{:S(2)}) copy-start(bf16[111,1024]{1,0:T(8,128)(2,1)} %copy-done.1) | copy-start | bytes 681988
  156.2 11.9 %copy-start.5 = (bf16[1,3,37,1024]{3,2,1,0:T(8,128)(2,1)S(1)}, bf16[1,3,37,1024]{3,2,1,0:T(8,128)(2,1)}, u32[]{:S(2)}) copy-start(bf16[1,3,37,1024]{3,2,1,0:T(8,128)(2,1)} %copy-done.4) | copy-start | bytes 681988
  156.2 8.2 %all-to-all-start.1 = ((bf16[2,111,512]{2,1,0:T(8,128)(2,1)}), bf16[2,111,512]{2,1,0:T(8,128)(2,1)S(1)}, u32[]{:S(2)}, u32[]{:S(2)}) async-start(bf16[2,111,512]{2,1,0:T(8,128)(2,1)} %copy.52), calls=%async_computation.1 | async-start | bytes 458752 | tf_op jit(solution)/shard_map/all_to_all | solution.py:132
  159.8 8.7 %copy-start.9 = (f32[2048]{0:T(1024)S(1)}, f32[2048]{0:T(1024)}, u32[]{:S(2)}) copy-start(f32[2048]{0:T(1024)} %param.20) | copy-start | bytes 24580
  159.8 8.7 %copy-start.10 = (f32[256]{0:T(256)S(1)}, f32[256]{0:T(256)}, u32[]{:S(2)}) copy-start(f32[256]{0:T(256)} %param.22) | copy-start | bytes 3076
  164.9 13.3 %copy-start.6 = (bf16[3,3,256,256]{3,2,1,0:T(8,128)(2,1)S(1)}, bf16[3,3,256,256]{3,2,1,0:T(8,128)(2,1)}, u32[]{:S(2)}) copy-start(bf16[3,3,256,256]{3,2,1,0:T(8,128)(2,1)} %param.23) | copy-start | bytes 3538948
  168.0 11.6 %copy-start.7 = (bf16[1,3,37,1024]{3,2,1,0:T(8,128)(2,1)}, bf16[1,3,37,1024]{3,2,1,0:T(8,128)(2,1)S(1)}, u32[]{:S(2)}) copy-start(bf16[1,3,37,1024]{3,2,1,0:T(8,128)(2,1)S(1)} %reshape.341) | copy-start | bytes 681988
  170.0 4.9 %collective-permute-start = (bf16[1,1,37,256]{3,2,1,0:T(8,128)(2,1)S(1)}, bf16[1,1,37,256]{3,2,1,0:T(8,128)(2,1)S(1)}, u32[]{:S(2)}, u32[]{:S(2)}) collective-permute-start(bf16[1,1,37,256]{3,2,1,0:T(8,128)(2,1)S(1)} %get-tuple-element.118), channel_id=1, source_target_pairs={{0,1},{1,2},{2,3},{4,5},{5,6},{6,7},{8,9},{9,10},{10,11},{12,13},{... | collective-permute-start | bytes 56840 | tf_op jit(solution)/shard_map/ppermute | solution.py:16
  173.0 5.1 %collective-permute-start.1 = (bf16[1,1,37,256]{3,2,1,0:T(8,128)(2,1)S(1)}, bf16[1,1,37,256]{3,2,1,0:T(8,128)(2,1)S(1)}, u32[]{:S(2)}, u32[]{:S(2)}) collective-permute-start(bf16[1,1,37,256]{3,2,1,0:T(8,128)(2,1)S(1)} %get-tuple-element.119), channel_id=1, source_target_pairs={{1,0},{2,1},{3,2},{5,4},{6,5},{7,6},{9,8},{10,9},{11,10},{13,12},{... | collective-permute-start | bytes 56840 | tf_op jit(solution)/shard_map/ppermute | solution.py:19
Sparse Core Ops, SparseCore 0:
  9.5 37.4 all-gather.8
  59.8 28.5 all-gather.12
  90.0 26.3 all-gather.14
  117.9 31.9 all-gather.10
